TPU v7x, 512 devices: a whole 4x8x8 slice. The times are simulated.
512 devices in a mesh: tile: 64 (over x, y, core), thick: 8 (over z).
Axes of the slice: x: 4, y: 8, z: 8, core: 2. Of those that a mesh axis runs over, the one named last changes fastest.
Arguments:
- velocity: float32 [3, 256, 128, 128], P(None, 'thick', 'tile'), may hold values from -6 to 6
- forcing: float32 [3, 256, 128, 128], P(None, 'thick', 'tile'), may hold values from -4 to 4
- viscosity: float32 [256, 128, 128], P('thick', 'tile'), may hold values from 0.1 to 1.6
- fibre: float32 [3, 256, 128, 128], P(None, 'thick', 'tile'), may hold values from -1.5 to 1.5
- inertia: float32 [256, 128, 128], P('thick', 'tile'), may hold values from 0.001 to 0.004
Outputs:
- update: float32 [3, 256, 128, 128], P(None, 'thick', 'tile')
- krylov_image: float32 [3, 256, 128, 128], P(None, 'thick', 'tile')
All inputs are finite; a program needn't handle non-finite values.
Results may differ from a plain program's by a relative error of at most 0.0003.
Values sent between devices are 32-bit elements; how exact they have to be, the bound alone decides.
A program may use at most 64 MiB of HBM per device.

v0:
```python
import functools

import jax
import jax.numpy as jnp
from jax import lax
from jax.experimental import pallas as pl
from jax.experimental.pallas import tpu as pltpu
from jax.sharding import PartitionSpec as P

MESH = pl.DeviceIdType.MESH
SLICES = 8
SYM = ((0, 1, 2), (1, 3, 4), (2, 4, 5))
TILE = (8, 128)


def roll_rows(values, shift):
    return values if shift % 8 == 0 else pltpu.roll(values, shift % 8, 0)


def row_ids():
    return lax.broadcasted_iota(jnp.int32, TILE, 0)


def load_slices(ref, lead=()):
    def one(v):
        halves = [ref[lead + (pl.ds(2 * v + x, 4, stride=16), slice(None))] for x in (0, 1)]
        return jnp.concatenate(halves, axis=0)

    return [one(v) for v in range(SLICES)]


def store_slices(ref, lead, slices):
    for v in range(SLICES):
        for x in (0, 1):
            ref[lead + (pl.ds(2 * v + x, 4, stride=16), slice(None))] = slices[v][4 * x : 4 * x + 4]


def pack_rows(fields, pos):
    rows = row_ids() % 4
    packed = roll_rows(fields[0], -pos)
    for j in range(1, len(fields)):
        packed = jnp.where(rows == j, roll_rows(fields[j], j - pos), packed)
    return packed


def pack_sides(left_ref, right_ref, fields):
    low = row_ids() < 4
    for j, slices in enumerate(fields):
        for m in range(4):
            first, second = slices[2 * m], slices[2 * m + 1]
            left_ref[4 * j + m] = jnp.where(low, first, roll_rows(second, 4))
            right_ref[4 * j + m] = jnp.where(low, roll_rows(first, 4), second)


def neighbours(tiles, groups):
    t, k = lax.axis_index("tile"), lax.axis_index("thick")
    left, right = lax.rem(t + tiles - 1, tiles), lax.rem(t + 1, tiles)
    down, up = lax.rem(k + groups - 1, groups), lax.rem(k + 1, groups)
    return [
        (left, k), (right, k), (t, up), (t, down),
        (right, up), (left, up), (right, down), (left, down),
    ]


def greet(targets):
    barrier = pltpu.get_barrier_semaphore()
    for target in targets:
        pl.semaphore_signal(barrier, inc=1, device_id=target, device_id_type=MESH)
    pl.semaphore_wait(barrier, len(targets))


def exchange(targets, sent, landed, send_sems, recv_sems):
    copies = [
        pltpu.make_async_remote_copy(
            src_ref=src, dst_ref=dst, send_sem=send_sems.at[i], recv_sem=recv_sems.at[i],
            device_id=target, device_id_type=MESH,
        )
        for i, (target, src, dst) in enumerate(zip(targets, sent, landed))
    ]
    for copy in copies:
        copy.start()
    for copy in copies:
        copy.wait()


def halo_out(tx_left, tx_right, tx_top, tx_bot):
    corner = tx_top.at[pl.ds(0, 1)]
    return [tx_left, tx_right, tx_top, tx_bot, corner, corner, tx_bot, tx_bot]


def halo_in(rx_left, rx_right, rx_below, rx_rest):
    rest = [rx_rest.at[pl.ds(i, 1)] for i in range(5)]
    return [rx_right, rx_left, rx_below] + rest


def first_halo_kernel(
    tiles, groups, vel, visc, fibre, rx_left, rx_right, rx_below, rx_rest,
    tx_left, tx_right, tx_top, tx_bot, send_sems, recv_sems,
):
    targets = neighbours(tiles, groups)
    fields = [load_slices(vel, (c,)) for c in range(3)] + [load_slices(visc)]
    pack_sides(tx_left, tx_right, fields)
    tx_bot[0] = pack_rows([f[0] for f in fields], 0)
    tx_top[0] = pack_rows([f[7] for f in fields], 3)
    tx_top[1] = pack_rows([load_slices(fibre, (c,))[7] for c in range(3)], 3)
    greet(targets)
    exchange(
        targets, halo_out(tx_left, tx_right, tx_top, tx_bot),
        halo_in(rx_left, rx_right, rx_below, rx_rest), send_sems, recv_sems,
    )


def second_halo_kernel(
    tiles, groups, update, rx_left, rx_right, rx_below, rx_rest,
    tx_left, tx_right, tx_top, tx_bot, send_sems, recv_sems,
):
    targets = neighbours(tiles, groups)
    fields = [load_slices(update, (c,)) for c in range(3)]
    pack_sides(tx_left, tx_right, fields)
    tx_bot[0] = pack_rows([f[0] for f in fields], 0)
    tx_top[0] = pack_rows([f[7] for f in fields], 3)
    greet(targets)
    exchange(
        targets, halo_out(tx_left, tx_right, tx_top, tx_bot),
        halo_in(rx_left, rx_right, rx_below, rx_rest), send_sems, recv_sems,
    )


def gather_kernel(groups, own, gathered, send_sems, recv_sems):
    t, k = lax.axis_index("tile"), lax.axis_index("thick")
    targets = [(t, lax.rem(k + d, groups)) for d in range(1, groups)]
    greet(targets)
    copies = [
        pltpu.make_async_remote_copy(
            src_ref=own, dst_ref=gathered.at[k], send_sem=send_sems.at[i], recv_sem=recv_sems.at[i],
            device_id=target, device_id_type=MESH,
        )
        for i, target in enumerate(targets)
    ]
    for copy in copies:
        copy.start()
    gathered[k] = own[...]
    for copy in copies:
        copy.wait()


def edges(tiles, groups):
    t, k = lax.axis_index("tile"), lax.axis_index("thick")
    rows = row_ids()
    low = rows < 4
    side_ok = jnp.logical_or(
        jnp.logical_and(low, t > 0), jnp.logical_and(jnp.logical_not(low), t < tiles - 1)
    )
    return rows, low, side_ok, k > 0, k < groups - 1


def below_slice(slices, packed, j, has_below, rows):
    inside = roll_rows(slices[7], 1)
    return jnp.where(rows % 4 == 0, jnp.where(has_below, roll_rows(packed, -j), 0.0), inside)


def above_slice(slices, packed, j, has_above, rows):
    inside = roll_rows(slices[0], -1)
    return jnp.where(rows % 4 == 3, jnp.where(has_above, roll_rows(packed, 3 - j), 0.0), inside)


def extended(slices, j, rx_left, rx_right, rx_below, rx_rest, place):
    rows, low, side_ok, has_below, has_above = place
    sides = []
    for m in range(4):
        left, right = rx_left[4 * j + m], rx_right[4 * j + m]
        sides.append(jnp.where(side_ok, jnp.where(low, left, roll_rows(right, 4)), 0.0))
        sides.append(jnp.where(side_ok, jnp.where(low, roll_rows(left, 4), right), 0.0))
    centre = (
        [below_slice(slices, rx_below[0], j, has_below, rows)]
        + slices
        + [above_slice(slices, rx_rest[0], j, has_above, rows)]
    )
    below = roll_rows(jnp.where(low, rx_rest[2], rx_rest[1]), 4 - j)
    above = roll_rows(jnp.where(low, rx_rest[4], rx_rest[3]), 7 - j)
    below = jnp.where(jnp.logical_and(side_ok, has_below), below, 0.0)
    above = jnp.where(jnp.logical_and(side_ok, has_above), above, 0.0)
    sides = (
        [jnp.where(rows % 4 == 0, below, roll_rows(sides[7], 1))]
        + sides
        + [jnp.where(rows % 4 == 3, above, roll_rows(sides[0], -1))]
    )
    return centre, sides


def smooth(centre, sides):
    lanes = lax.broadcasted_iota(jnp.int32, TILE, 1)
    across = [c + 0.5 * (roll_rows(c, 4) + s) for c, s in zip(centre, sides)]
    out = []
    for v in range(SLICES):
        z = across[v + 1] + 0.5 * (across[v] + across[v + 2])
        up = jnp.where(lanes < 127, pltpu.roll(z, 127, 1), 0.0)
        down = jnp.where(lanes > 0, pltpu.roll(z, 1, 1), 0.0)
        out.append(z + 0.5 * (up + down))
    return out


def stencil(field, visc, weight):
    centre, sides = field
    visc_centre, visc_sides = visc
    flat = smooth(centre, sides)
    scaled = smooth(
        [a * b for a, b in zip(visc_centre, centre)], [a * b for a, b in zip(visc_sides, sides)]
    )
    return [
        (1.0 / 3.0) * (centre[v + 1] * weight[v] - visc_centre[v + 1] * flat[v] - scaled[v])
        for v in range(SLICES)
    ]


def stencil_weight(visc):
    flat = smooth(*visc)
    return [8.0 * visc[0][v + 1] + flat[v] for v in range(SLICES)]


def sym_inverse(d):
    a, b, c, e, f, g = d
    c00, c01, c02 = e * g - f * f, c * f - b * g, b * f - c * e
    r = 1.0 / (a * c00 + b * c01 + c * c02)
    return [r * q for q in (c00, c01, c02, a * g - c * c, b * c - a * f, a * e - b * b)]


def dot3(xs, ys):
    return xs[0] * ys[0] + xs[1] * ys[1] + xs[2] * ys[2]


def mat_vec(m, x):
    return [dot3(m[i], x) for i in range(3)]


def mat_mat(m, n):
    return [[dot3(m[i], [n[0][j], n[1][j], n[2][j]]) for j in range(3)] for i in range(3)]


def sym_product(m, n):
    return [dot3(m[i], [n[0][j], n[1][j], n[2][j]]) for i in range(3) for j in range(i, 3)]


def transposed(m):
    return [[m[j][i] for j in range(3)] for i in range(3)]


def full(d):
    return [[d[SYM[i][j]] for j in range(3)] for i in range(3)]


def eliminate(diag, source, to_prev, next_to):
    inv = full(sym_inverse(diag))
    pm = mat_mat(inv, to_prev)
    qm = mat_mat(inv, transposed(next_to))
    y = mat_vec(inv, source)
    prev_t = transposed(to_prev)
    return (
        (y, pm, qm),
        (sym_product(prev_t, pm), mat_vec(prev_t, y)),
        (sym_product(next_to, qm), mat_vec(next_to, y), mat_mat(next_to, pm)),
    )


def back(solved, x_prev, x_next):
    y, pm, qm = solved
    return [y[i] + dot3(pm[i], x_prev) + dot3(qm[i], x_next) for i in range(3)]


def minus(a, b):
    return [x - y for x, y in zip(a, b)]


def plus(a, b):
    return [x + y for x, y in zip(a, b)]


def select(mask, a, b):
    return [jnp.where(mask, x, y) for x, y in zip(a, b)]


def keep(mask, a):
    return [jnp.where(mask, x, 0.0) for x in a]


def moved(a, shift):
    return [roll_rows(x, shift) for x in a]


def moved_mat(m, shift):
    return [moved(r, shift) for r in m]


def reduce_rows(diag, source, link, pos):
    even = pos % 2 == 0
    done4, to_p, to_n = eliminate(diag, source, link, moved_mat(link, -1))
    base_d, base_s = keep(pos == 0, to_p[0]), keep(pos == 0, to_p[1])
    one = pos == 1
    diag = minus(diag, plus(moved(to_n[0], 1), keep(one, moved(to_p[0], -1))))
    source = plus(source, plus(moved(to_n[1], 1), keep(one, moved(to_p[1], -1))))
    link = moved_mat(to_n[2], 1)
    done5, to_p, to_n = eliminate(diag, source, link, moved_mat(link, -2))
    zero = pos == 0
    base_d = plus(base_d, keep(zero, moved(to_p[0], -1)))
    base_s = plus(base_s, keep(zero, moved(to_p[1], -1)))
    diag = minus(diag, moved(to_n[0], 2))
    source = plus(source, moved(to_n[1], 2))
    link = moved_mat(to_n[2], 2)
    return done4, done5, base_d, base_s, diag, source, link


def expand_rows(done4, done5, x_base, x_last, pos):
    x_one = back(done5, moved(x_base, 1), moved(x_last, -2))
    kept = select(pos == 1, x_one, x_last)
    x_even = back(done4, select(pos == 0, x_base, moved(kept, 1)), moved(kept, -1))
    return select(pos % 2 == 0, x_even, kept)


def flat_done(done):
    y, pm, qm = done
    return list(y) + [e for r in pm for e in r] + [e for r in qm for e in r]


def unflat_done(ref, i):
    e = [ref[i, j] for j in range(21)]
    return e[0:3], [e[3:6], e[6:9], e[9:12]], [e[12:15], e[15:18], e[18:21]]


def local_kernel(
    tiles, groups, vel, forcing, visc, fibre, inertia, rx_left, rx_right, rx_below, rx_rest,
    reduced, stash,
):
    place = edges(tiles, groups)
    rows, low, side_ok, has_below, has_above = place
    pos = rows % 4
    halo = (rx_left, rx_right, rx_below, rx_rest, place)
    visc_ext = extended(load_slices(visc), 3, *halo)
    weight = stencil_weight(visc_ext)
    source = [[] for _ in range(SLICES)]
    for c in range(3):
        image = stencil(extended(load_slices(vel, (c,)), c, *halo), visc_ext, weight)
        force = load_slices(forcing, (c,))
        for v in range(SLICES):
            source[v].append(force[v] - image[v])
    fib = [load_slices(fibre, (c,)) for c in range(3)]
    fib = [[below_slice(fib[c], rx_below[1], c, has_below, rows)] + fib[c] for c in range(3)]
    centre = visc_ext[0]
    face = []
    for v in range(SLICES + 1):
        mu = 0.5 * (centre[v] + centre[v + 1])
        f = [fib[c][v] for c in range(3)]
        g = [mu * q for q in f]
        face.append(
            [mu + g[0] * f[0], g[0] * f[1], g[0] * f[2], mu + g[1] * f[1], g[1] * f[2], mu + g[2] * f[2]]
        )
    mass = load_slices(inertia)
    diag, link = [], []
    for v in range(SLICES):
        d = plus(face[v], face[v + 1])
        m = mass[v] * centre[v + 1]
        for i in (0, 3, 5):
            d[i] = d[i] + m
        diag.append(d)
        link.append(full(face[v]))
    joined = jnp.logical_or(pos > 0, has_below)
    link[0] = [keep(joined, r) for r in link[0]]
    done = []
    low_d, low_s = None, None
    for step in (1, 2, 4):
        for e in range(step - 1, SLICES - 1, 2 * step):
            n, p = e + step, e - step
            solved, to_p, to_n = eliminate(diag[e], source[e], link[e], link[n])
            done.append(solved)
            diag[n], source[n], link[n] = minus(diag[n], to_n[0]), plus(source[n], to_n[1]), to_n[2]
            if p >= 0:
                diag[p], source[p] = minus(diag[p], to_p[0]), plus(source[p], to_p[1])
            elif low_d is None:
                low_d, low_s = to_p
            else:
                low_d, low_s = plus(low_d, to_p[0]), plus(low_s, to_p[1])
    inner = pos < 3
    d7 = minus(diag[7], keep(inner, moved(low_d, -1)))
    s7 = plus(source[7], keep(inner, moved(low_s, -1)))
    done4, done5, base_d, base_s, last_d, last_s, last_l = reduce_rows(d7, s7, link[7], pos)
    done += [done4, done5]
    base_d, base_s = plus(base_d, low_d), plus(base_s, low_s)
    out = moved(base_d, 3) + moved(base_s, 3) + last_d + last_s + [e for r in last_l for e in r]
    for i in range(7):
        reduced[i] = pack_rows(out[4 * i : 4 * i + 4], 3)
    for i, solved in enumerate(done):
        for j, e in enumerate(flat_done(solved)):
            stash[i, j] = e


def solve_kernel(groups, gathered, stash, update):
    k = lax.axis_index("thick")
    pos = row_ids() % 4

    def field(f, h):
        value = None
        for s in range(4):
            part = roll_rows(gathered[2 * s + h, f // 4], s - f % 4)
            value = part if value is None else jnp.where(pos == s, part, value)
        return value

    def fields(lo, hi, h):
        return [field(f, h) for f in range(lo, hi)]

    def link_of(h):
        e = fields(18, 27, h)
        return [e[0:3], e[3:6], e[6:9]]

    inner = pos < 3
    d0 = minus(fields(9, 15, 0), fields(0, 6, 1))
    s0 = plus(fields(15, 18, 0), fields(6, 9, 1))
    d1 = minus(fields(9, 15, 1), keep(inner, moved(fields(0, 6, 0), -1)))
    s1 = plus(fields(15, 18, 1), keep(inner, moved(fields(6, 9, 0), -1)))
    done_h, to_p, to_n = eliminate(d0, s0, link_of(0), link_of(1))
    d1 = minus(minus(d1, to_n[0]), keep(inner, moved(to_p[0], -1)))
    s1 = plus(plus(s1, to_n[1]), keep(inner, moved(to_p[1], -1)))
    done4, done5, _, _, last_d, last_s, _ = reduce_rows(d1, s1, to_n[2], pos)
    x_last = mat_vec(full(sym_inverse(last_d)), last_s)
    nothing = [jnp.zeros(TILE, jnp.float32)] * 3
    x1 = expand_rows(done4, done5, nothing, x_last, pos)
    x0 = back(done_h, keep(pos > 0, moved(x1, 1)), x1)
    own, base = nothing, nothing
    for g in range(groups):
        x = (x0, x1)[g % 2]
        own = select(k == g, moved(x, 3 - g // 2), own)
        base = select(k == g + 1, moved(x, -(g // 2)), base)
    done = [unflat_done(stash, i) for i in range(9)]
    x = [None] * SLICES
    x[7] = expand_rows(done[7], done[8], base, own, pos)
    under = select(pos == 0, base, moved(x[7], 1))
    x[3] = back(done[6], under, x[7])
    x[1] = back(done[4], under, x[3])
    x[5] = back(done[5], x[3], x[7])
    x[0] = back(done[0], under, x[1])
    for i, v in enumerate((2, 4, 6)):
        x[v] = back(done[1 + i], x[v - 1], x[v + 1])
    for c in range(3):
        store_slices(update, (c,), [x[v][c] for v in range(SLICES)])


def image_kernel(
    tiles, groups, update, visc, v_left, v_right, v_below, v_rest,
    rx_left, rx_right, rx_below, rx_rest, image,
):
    place = edges(tiles, groups)
    visc_ext = extended(load_slices(visc), 3, v_left, v_right, v_below, v_rest, place)
    weight = stencil_weight(visc_ext)
    for c in range(3):
        field = extended(
            load_slices(update, (c,)), c, rx_left, rx_right, rx_below, rx_rest, place
        )
        store_slices(image, (c,), stencil(field, visc_ext, weight))


def tiles_of(count):
    return jax.ShapeDtypeStruct((count,) + TILE, jnp.float32)


def call(kernel, name, out_shape, scratch=(), collective_id=None):
    vmem = pl.BlockSpec(memory_space=pltpu.VMEM)

    def run(*operands):
        return pl.pallas_call(
            kernel,
            out_shape=out_shape,
            in_specs=[vmem] * len(operands),
            out_specs=jax.tree.map(lambda _: vmem, out_shape),
            scratch_shapes=list(scratch),
            compiler_params=pltpu.CompilerParams(
                collective_id=collective_id, has_side_effects=collective_id is not None,
                vmem_limit_bytes=16 * 1024 * 1024,
            ),
            name=name,
        )(*operands)

    return run


def halo_call(kernel, name, fields, top, collective_id):
    sides = 4 * fields
    buffers = [pltpu.VMEM((n,) + TILE, jnp.float32) for n in (sides, sides, top, 1)]
    sems = [pltpu.SemaphoreType.DMA((8,)), pltpu.SemaphoreType.DMA((8,))]
    out = [tiles_of(n) for n in (sides, sides, top, 5)]
    return call(kernel, name, out, buffers + sems, collective_id)


def per_device(tiles, groups, velocity, forcing, viscosity, fibre, inertia):
    vel, force, fib = (a.reshape(3, 64, 128) for a in (velocity, forcing, fibre))
    visc, mass = viscosity.reshape(64, 128), inertia.reshape(64, 128)
    bind = functools.partial
    halo = halo_call(bind(first_halo_kernel, tiles, groups), "halo_a", 4, 2, 0)(vel, visc, fib)
    stash_shape = jax.ShapeDtypeStruct((9, 21) + TILE, jnp.float32)
    reduced, stash = call(bind(local_kernel, tiles, groups), "local", [tiles_of(7), stash_shape])(
        vel, force, visc, fib, mass, *halo
    )
    sems = [pltpu.SemaphoreType.DMA((groups - 1,)), pltpu.SemaphoreType.DMA((groups - 1,))]
    gathered_shape = jax.ShapeDtypeStruct((groups, 7) + TILE, jnp.float32)
    gathered = call(bind(gather_kernel, groups), "gather", gathered_shape, sems, 1)(reduced)
    block = jax.ShapeDtypeStruct((3, 64, 128), jnp.float32)
    update = call(bind(solve_kernel, groups), "solve", block)(gathered, stash)
    halo2 = halo_call(bind(second_halo_kernel, tiles, groups), "halo_b", 3, 1, 2)(update)
    image = call(bind(image_kernel, tiles, groups), "image", block)(update, visc, *halo, *halo2)
    return update.reshape(velocity.shape), image.reshape(velocity.shape)


def solution(mesh):
    wide, flat = P(None, "thick", "tile", None), P("thick", "tile", None)
    return jax.shard_map(
        functools.partial(per_device, mesh.shape["tile"], mesh.shape["thick"]),
        mesh=mesh,
        in_specs=(wide, wide, flat, wide, flat),
        out_specs=(wide, wide),
        check_vma=False,
    )
```

profile of v0, /device:TPU:1, one launch (start us, length us, event | category | flops | bytes accessed | tf_op | source)
XLA Modules:
  0.0 44.7 jit_solution(7929473097954377391)
XLA Ops:
  0.6 0.0 copy-start.2
  0.6 0.9 %copy-done.2 = f32[3,32,2,128]{3,2,1,0:T(2,128)S(1)} copy-done((f32[3,32,2,128]{3,2,1,0:T(2,128)S(1)}, f32[3,32,2,128]{3,2,1,0:T(2,128)}, u32[]{:S(2)}) %copy-start.2) | copy-done | bytes 98328
  1.5 0.0 copy-start.3
  1.5 0.9 %copy-done.3 = f32[3,32,2,128]{3,2,1,0:T(2,128)S(1)} copy-done((f32[3,32,2,128]{3,2,1,0:T(2,128)S(1)}, f32[3,32,2,128]{3,2,1,0:T(2,128)}, u32[]{:S(2)}) %copy-start.3) | copy-done | bytes 98328
  2.4 0.0 copy-start.4
  2.4 0.8 %copy-done.4 = f32[32,2,128]{2,1,0:T(2,128)S(1)} copy-done((f32[32,2,128]{2,1,0:T(2,128)S(1)}, f32[32,2,128]{2,1,0:T(2,128)}, u32[]{:S(2)}) %copy-start.4) | copy-done | bytes 32792
  3.2 0.0 copy-start.6
  3.2 0.0 copy-start.7
  3.2 18.0 %halo_a.1 = (f32[16,8,128]{2,1,0:T(8,128)S(1)}, f32[16,8,128]{2,1,0:T(8,128)S(1)}, f32[2,8,128]{2,1,0:T(8,128)S(1)}, f32[5,8,128]{2,1,0:T(8,128)S(1)}) custom-call(f32[3,64,128]{2,1,0:T(8,128)S(1)} %bitcast.8, f32[64,128]{1,0:T(8,128)S(1)} %bitcast.12, f32[3,64,128]{2,1,0:T(8,128)S(1)} %bitcast.10), custom_call_target="tpu_custom_call" | custom-call | tf_op jit(solution)/shard_map/halo_a/pallas_call | solution.py:467
  21.1 0.0 copy-done.6
  21.2 0.0 copy-done.7
  21.2 0.7 %local.1 = (f32[7,8,128]{2,1,0:T(8,128)S(1)}, f32[9,21,8,128]{3,2,1,0:T(8,128)S(1)}) custom-call(f32[3,64,128]{2,1,0:T(8,128)S(1)} %bitcast.9, f32[3,64,128]{2,1,0:T(8,128)S(1)} %bitcast.15, f32[64,128]{1,0:T(8,128)S(1)} %bitcast.13, f32[3,64,128]{2,1,0:T(8,128)S(1)} %bitcast.11, f32[64,128]{1,0:T(8,128)S(1)} %bitcast.16, ...), custom_call_target="tpu_custom_call" | custom-call | tf_op jit(solution)/shard_map/local/pallas_call | solution.py:467
  21.8 10.7 %gather.1.gathered = f32[8,7,8,128]{3,2,1,0:T(8,128)S(1)} custom-call(f32[7,8,128]{2,1,0:T(8,128)S(1)} %get-tuple-element.16.own), custom_call_target="tpu_custom_call" | custom-call | tf_op jit(solution)/shard_map/gather/pallas_call | solution.py:467
  32.5 0.0 copy-start.5
  32.5 0.9 %solve.1.update = f32[3,64,128]{2,1,0:T(8,128)} custom-call(f32[8,7,8,128]{3,2,1,0:T(8,128)S(1)} %gather.1.gathered, f32[9,21,8,128]{3,2,1,0:T(8,128)S(1)} %get-tuple-element.17.stash), custom_call_target="tpu_custom_call" | custom-call | tf_op jit(solution)/shard_map/solve/pallas_call | solution.py:467
  33.4 0.0 copy-start
  33.4 0.9 %copy-done = f32[3,64,128]{2,1,0:T(8,128)S(1)} copy-done((f32[3,64,128]{2,1,0:T(8,128)S(1)}, f32[3,64,128]{2,1,0:T(8,128)}, u32[]{:S(2)}) %copy-start) | copy-done | bytes 98328
  34.3 0.0 copy-start.1
  34.3 9.5 %halo_b.1 = (f32[12,8,128]{2,1,0:T(8,128)S(1)}, f32[12,8,128]{2,1,0:T(8,128)S(1)}, f32[1,8,128]{2,1,0:T(8,128)S(1)}, f32[5,8,128]{2,1,0:T(8,128)S(1)}) custom-call(f32[3,64,128]{2,1,0:T(8,128)S(1)} %copy-done), custom_call_target="tpu_custom_call" | custom-call | tf_op jit(solution)/shard_map/halo_b/pallas_call | solution.py:467
  43.8 0.0 copy-done.5
  43.8 0.0 copy-done.1
  43.8 0.9 %image.1 = f32[3,64,128]{2,1,0:T(8,128)} custom-call(f32[3,64,128]{2,1,0:T(8,128)S(1)} %copy-done.1, f32[64,128]{1,0:T(8,128)S(1)} %bitcast.14, f32[16,8,128]{2,1,0:T(8,128)S(1)} %get-tuple-element.12.rx_left.v_left, f32[16,8,128]{2,1,0:T(8,128)S(1)} %get-tuple-element.13.rx_right.v_right, f32[2,8,128]{2,1,0:T(8,128)S(1)} %get-tuple-element.14.rx_below.v_below, ...), custom_call_target="tpu_custom_call" | custom-call | tf_op jit(solution)/shard_map/image/pallas_call | solution.py:467
Async XLA Ops:
  0.6 0.9 %copy-start.2 = (f32[3,32,2,128]{3,2,1,0:T(2,128)S(1)}, f32[3,32,2,128]{3,2,1,0:T(2,128)}, u32[]{:S(2)}) copy-start(f32[3,32,2,128]{3,2,1,0:T(2,128)} %param.5) | copy-start | bytes 294916
  1.5 0.9 %copy-start.3 = (f32[3,32,2,128]{3,2,1,0:T(2,128)S(1)}, f32[3,32,2,128]{3,2,1,0:T(2,128)}, u32[]{:S(2)}) copy-start(f32[3,32,2,128]{3,2,1,0:T(2,128)} %param.8) | copy-start | bytes 294916
  2.4 0.8 %copy-start.4 = (f32[32,2,128]{2,1,0:T(2,128)S(1)}, f32[32,2,128]{2,1,0:T(2,128)}, u32[]{:S(2)}) copy-start(f32[32,2,128]{2,1,0:T(2,128)} %param.7) | copy-start | bytes 98308
  3.2 18.0 %copy-start.6 = (f32[3,32,2,128]{3,2,1,0:T(2,128)S(1)}, f32[3,32,2,128]{3,2,1,0:T(2,128)}, u32[]{:S(2)}) copy-start(f32[3,32,2,128]{3,2,1,0:T(2,128)} %param.6) | copy-start | bytes 294916
  3.2 18.0 %copy-start.7 = (f32[32,2,128]{2,1,0:T(2,128)S(1)}, f32[32,2,128]{2,1,0:T(2,128)}, u32[]{:S(2)}) copy-start(f32[32,2,128]{2,1,0:T(2,128)} %param.9) | copy-start | bytes 98308
  32.5 11.3 %copy-start.5 = (f32[32,2,128]{2,1,0:T(2,128)S(1)}, f32[32,2,128]{2,1,0:T(2,128)}, u32[]{:S(2)}) copy-start(f32[32,2,128]{2,1,0:T(2,128)} %param.7) | copy-start | bytes 98308
  33.4 0.9 %copy-start = (f32[3,64,128]{2,1,0:T(8,128)S(1)}, f32[3,64,128]{2,1,0:T(8,128)}, u32[]{:S(2)}) copy-start(f32[3,64,128]{2,1,0:T(8,128)} %solve.1.update) | copy-start | bytes 294916
  34.3 9.5 %copy-start.1 = (f32[3,64,128]{2,1,0:T(8,128)S(1)}, f32[3,64,128]{2,1,0:T(8,128)}, u32[]{:S(2)}) copy-start(f32[3,64,128]{2,1,0:T(8,128)} %solve.1.update) | copy-start | bytes 294916
where the time goes:
time: 45 us; the launch traced here: 44.7 us
  Pallas kernels  40.5 us (90%)
  local copies, waits for them, and re-layouts  3.44 us (8%)
  between operations  0.71 us (2%)
    pallas_call x6, Pallas kernels, run(): pl.pallas_call(kernel, out_shape=out_shape, in_specs=[vmem] * len(operand...  40.5 us
    unnamed x16, local copies, waits for them, and re-layouts  3.44 us

commit v1 on v0

v1 whole, which is shorter than its diff:
```python
import functools

import jax
import jax.numpy as jnp
from jax import lax
from jax.experimental import pallas as pl
from jax.experimental.pallas import tpu as pltpu
from jax.sharding import PartitionSpec as P

MESH = pl.DeviceIdType.MESH
SLICES = 8
SYM = ((0, 1, 2), (1, 3, 4), (2, 4, 5))
TILE = (8, 128)


def roll_rows(values, shift):
    return values if shift % 8 == 0 else pltpu.roll(values, shift % 8, 0)


def row_ids():
    return lax.broadcasted_iota(jnp.int32, TILE, 0)


def load_slices(ref, lead=()):
    def one(v):
        halves = [ref[lead + (pl.ds(2 * v + x, 4, stride=16), slice(None))] for x in (0, 1)]
        return jnp.concatenate(halves, axis=0)

    return [one(v) for v in range(SLICES)]


def store_slices(ref, lead, slices):
    for v in range(SLICES):
        for x in (0, 1):
            ref[lead + (pl.ds(2 * v + x, 4, stride=16), slice(None))] = slices[v][4 * x : 4 * x + 4]


def pack_rows(fields, pos):
    rows = row_ids() % 4
    packed = roll_rows(fields[0], -pos)
    for j in range(1, len(fields)):
        packed = jnp.where(rows == j, roll_rows(fields[j], j - pos), packed)
    return packed


def pack_sides(left_ref, right_ref, fields):
    low = row_ids() < 4
    for j, slices in enumerate(fields):
        for m in range(4):
            first, second = slices[2 * m], slices[2 * m + 1]
            left_ref[4 * j + m] = jnp.where(low, first, roll_rows(second, 4))
            right_ref[4 * j + m] = jnp.where(low, roll_rows(first, 4), second)


def greet(targets):
    barrier = pltpu.get_barrier_semaphore()
    count = 0
    for target, there in targets:
        if there is None:
            pl.semaphore_signal(barrier, inc=1, device_id=target, device_id_type=MESH)
            count = count + 1
        else:

            @pl.when(there)
            def _():
                pl.semaphore_signal(barrier, inc=1, device_id=target, device_id_type=MESH)

            count = count + there.astype(jnp.int32)
    return lambda: pl.semaphore_wait(barrier, count)


def remote(src, dst, send_sem, recv_sem, target):
    return pltpu.make_async_remote_copy(
        src_ref=src, dst_ref=dst, send_sem=send_sem, recv_sem=recv_sem,
        device_id=target, device_id_type=MESH,
    )


def when(there, action):
    pl.when(there)(lambda: action())


def edges(tiles, groups):
    t, k = lax.axis_index("tile"), lax.axis_index("thick")
    rows = row_ids()
    low = rows < 4
    side_ok = jnp.logical_or(
        jnp.logical_and(low, t > 0), jnp.logical_and(jnp.logical_not(low), t < tiles - 1)
    )
    return rows, low, side_ok, k > 0, k < groups - 1


def below_slice(slices, packed, j, has_below, rows):
    inside = roll_rows(slices[7], 1)
    return jnp.where(rows % 4 == 0, jnp.where(has_below, roll_rows(packed, -j), 0.0), inside)


def above_slice(slices, packed, j, has_above, rows):
    inside = roll_rows(slices[0], -1)
    return jnp.where(rows % 4 == 3, jnp.where(has_above, roll_rows(packed, 3 - j), 0.0), inside)


def extended(slices, j, rx_left, rx_right, rx_below, rx_rest, place):
    rows, low, side_ok, has_below, has_above = place
    sides = []
    for m in range(4):
        left, right = rx_left[4 * j + m], rx_right[4 * j + m]
        sides.append(jnp.where(side_ok, jnp.where(low, left, roll_rows(right, 4)), 0.0))
        sides.append(jnp.where(side_ok, jnp.where(low, roll_rows(left, 4), right), 0.0))
    centre = (
        [below_slice(slices, rx_below[0], j, has_below, rows)]
        + slices
        + [above_slice(slices, rx_rest[0], j, has_above, rows)]
    )
    below = roll_rows(jnp.where(low, rx_rest[2], rx_rest[1]), 4 - j)
    above = roll_rows(jnp.where(low, rx_rest[4], rx_rest[3]), 7 - j)
    below = jnp.where(jnp.logical_and(side_ok, has_below), below, 0.0)
    above = jnp.where(jnp.logical_and(side_ok, has_above), above, 0.0)
    sides = (
        [jnp.where(rows % 4 == 0, below, roll_rows(sides[7], 1))]
        + sides
        + [jnp.where(rows % 4 == 3, above, roll_rows(sides[0], -1))]
    )
    return centre, sides


def smooth(centre, sides):
    lanes = lax.broadcasted_iota(jnp.int32, TILE, 1)
    across = [c + 0.5 * (roll_rows(c, 4) + s) for c, s in zip(centre, sides)]
    out = []
    for v in range(SLICES):
        z = across[v + 1] + 0.5 * (across[v] + across[v + 2])
        up = jnp.where(lanes < 127, pltpu.roll(z, 127, 1), 0.0)
        down = jnp.where(lanes > 0, pltpu.roll(z, 1, 1), 0.0)
        out.append(z + 0.5 * (up + down))
    return out


def stencil(field, visc, weight):
    centre, sides = field
    visc_centre, visc_sides = visc
    flat = smooth(centre, sides)
    scaled = smooth(
        [a * b for a, b in zip(visc_centre, centre)], [a * b for a, b in zip(visc_sides, sides)]
    )
    return [
        (1.0 / 3.0) * (centre[v + 1] * weight[v] - visc_centre[v + 1] * flat[v] - scaled[v])
        for v in range(SLICES)
    ]


def stencil_weight(visc):
    flat = smooth(*visc)
    return [8.0 * visc[0][v + 1] + flat[v] for v in range(SLICES)]


def sym_inverse(d):
    a, b, c, e, f, g = d
    c00, c01, c02 = e * g - f * f, c * f - b * g, b * f - c * e
    r = 1.0 / (a * c00 + b * c01 + c * c02)
    return [r * q for q in (c00, c01, c02, a * g - c * c, b * c - a * f, a * e - b * b)]


def dot3(xs, ys):
    return xs[0] * ys[0] + xs[1] * ys[1] + xs[2] * ys[2]


def mat_vec(m, x):
    return [dot3(m[i], x) for i in range(3)]


def mat_mat(m, n):
    return [[dot3(m[i], [n[0][j], n[1][j], n[2][j]]) for j in range(3)] for i in range(3)]


def sym_product(m, n):
    return [dot3(m[i], [n[0][j], n[1][j], n[2][j]]) for i in range(3) for j in range(i, 3)]


def transposed(m):
    return [[m[j][i] for j in range(3)] for i in range(3)]


def full(d):
    return [[d[SYM[i][j]] for j in range(3)] for i in range(3)]


def eliminate(diag, to_prev, next_to):
    inv = full(sym_inverse(diag))
    pm = mat_mat(inv, to_prev)
    qm = mat_mat(inv, transposed(next_to))
    to_p = sym_product(transposed(to_prev), pm)
    return (inv, pm, qm), to_p, sym_product(next_to, qm), mat_mat(next_to, pm)


def push(done, source):
    inv, pm, qm = done
    return mat_vec(inv, source), mat_vec(transposed(pm), source), mat_vec(transposed(qm), source)


def back(done, y, x_prev, x_next):
    _, pm, qm = done
    return [y[i] + dot3(pm[i], x_prev) + dot3(qm[i], x_next) for i in range(3)]


def minus(a, b):
    return [x - y for x, y in zip(a, b)]


def plus(a, b):
    return [x + y for x, y in zip(a, b)]


def select(mask, a, b):
    return [jnp.where(mask, x, y) for x, y in zip(a, b)]


def keep(mask, a):
    return [jnp.where(mask, x, 0.0) for x in a]


def moved(a, shift):
    return [roll_rows(x, shift) for x in a]


def moved_mat(m, shift):
    return [moved(r, shift) for r in m]


def reduce_matrix(diag, link, pos):
    done4, to_p, to_n, passed = eliminate(diag, link, moved_mat(link, -1))
    base = keep(pos == 0, to_p)
    diag = minus(diag, plus(moved(to_n, 1), keep(pos == 1, moved(to_p, -1))))
    link = moved_mat(passed, 1)
    done5, to_p, to_n, passed = eliminate(diag, link, moved_mat(link, -2))
    base = plus(base, keep(pos == 0, moved(to_p, -1)))
    return done4, done5, base, minus(diag, moved(to_n, 2)), moved_mat(passed, 2)


def reduce_source(done4, done5, source, pos):
    y4, to_p, to_n = push(done4, source)
    base = keep(pos == 0, to_p)
    source = plus(source, plus(moved(to_n, 1), keep(pos == 1, moved(to_p, -1))))
    y5, to_p, to_n = push(done5, source)
    base = plus(base, keep(pos == 0, moved(to_p, -1)))
    return y4, y5, base, plus(source, moved(to_n, 2))


def expand_rows(done4, done5, y4, y5, x_base, x_last, pos):
    x_one = back(done5, y5, moved(x_base, 1), moved(x_last, -2))
    kept = select(pos == 1, x_one, x_last)
    x_even = back(done4, y4, select(pos == 0, x_base, moved(kept, 1)), moved(kept, -1))
    return select(pos % 2 == 0, x_even, kept)


ORDER = ((1, 0), (1, 2), (1, 4), (1, 6), (2, 1), (2, 5), (4, 3))


def solve_kernel(
    tiles, groups, vel_in, force_in, visc_in, fibre_in, mass_in,
    update, ends, visc_out, rx_left, rx_right,
    vel, force, visc, fibre, mass, tx_left, tx_right, tx_top, tx_bot,
    h_left, h_right, h_below, h_rest, matrix_own, matrix_all, source_own, source_all,
    ux_left, ux_right, load_sems, halo_send, halo_recv, mat_send, mat_recv, src_send, src_recv,
    upd_send, upd_recv,
):
    t, k = lax.axis_index("tile"), lax.axis_index("thick")
    loads = [
        pltpu.make_async_copy(src, dst, load_sems.at[i])
        for i, (src, dst) in enumerate(
            ((visc_in, visc), (fibre_in, fibre), (vel_in, vel), (mass_in, mass), (force_in, force))
        )
    ]
    for load in loads:
        load.start()
    has_left, has_right, has_down, has_up = t > 0, t < tiles - 1, k > 0, k < groups - 1
    left, right = jnp.maximum(t - 1, 0), jnp.minimum(t + 1, tiles - 1)
    down, up = jnp.maximum(k - 1, 0), jnp.minimum(k + 1, groups - 1)
    both = jnp.logical_and
    peers = [(t, lax.rem(k + d, groups)) for d in range(1, groups)]
    corner = tx_top.at[pl.ds(0, 1)]
    rest = [h_rest.at[pl.ds(i, 1)] for i in range(5)]
    plan = [
        ((t, up), has_up, has_down, tx_top, h_below),
        ((t, down), has_down, has_up, tx_bot, rest[0]),
        ((left, k), has_left, has_right, tx_left, h_right),
        ((right, k), has_right, has_left, tx_right, h_left),
        ((right, up), both(has_right, has_up), both(has_left, has_down), corner, rest[1]),
        ((left, up), both(has_left, has_up), both(has_right, has_down), corner, rest[2]),
        ((right, down), both(has_right, has_down), both(has_left, has_up), tx_bot, rest[3]),
        ((left, down), both(has_left, has_down), both(has_right, has_up), tx_bot, rest[4]),
    ]
    all_here = greet([(p[0], p[1]) for p in plan[2:]] + [(p, None) for p in peers])
    halo = [
        (there, comes, remote(src, dst, halo_send.at[i], halo_recv.at[i], target))
        for i, (target, there, comes, src, dst) in enumerate(plan)
    ]
    for load in loads[:3]:
        load.wait()
    visc_c = load_slices(visc)
    fib = [load_slices(fibre, (c,)) for c in range(3)]
    v_c = [load_slices(vel, (c,)) for c in range(3)]
    fields = v_c + [visc_c]
    tx_bot[0] = pack_rows([f[0] for f in fields], 0)
    tx_top[0] = pack_rows([f[7] for f in fields], 3)
    tx_top[1] = pack_rows([f[7] for f in fib], 3)
    pack_sides(tx_left, tx_right, fields)
    all_here()
    for there, _, copy in halo:
        when(there, copy.start)
    place = edges(tiles, groups)
    rows, low, side_ok, has_below, has_above = place
    pos = rows % 4
    inner = pos < 3
    loads[3].wait()
    loads[4].wait()
    mass_c = load_slices(mass)
    for _, comes, copy in halo[:2]:
        when(comes, copy.wait_recv)
    centre = (
        [below_slice(visc_c, h_below[0], 3, has_below, rows)]
        + visc_c
        + [above_slice(visc_c, h_rest[0], 3, has_above, rows)]
    )
    fib = [[below_slice(fib[c], h_below[1], c, has_below, rows)] + fib[c] for c in range(3)]
    face = []
    for v in range(SLICES + 1):
        mu = 0.5 * (centre[v] + centre[v + 1])
        f = [fib[c][v] for c in range(3)]
        g = [mu * q for q in f]
        face.append(
            [mu + g[0] * f[0], g[0] * f[1], g[0] * f[2], mu + g[1] * f[1], g[1] * f[2], mu + g[2] * f[2]]
        )
    diag, link = [], []
    for v in range(SLICES):
        d = plus(face[v], face[v + 1])
        m = mass_c[v] * centre[v + 1]
        for i in (0, 3, 5):
            d[i] = d[i] + m
        diag.append(d)
        link.append(full(face[v]))
    top_diag = diag[7]
    joined = jnp.logical_or(pos > 0, has_below)
    link[0] = [keep(joined, r) for r in link[0]]
    done = []
    low_d = None
    for step, e in ORDER:
        n, p = e + step, e - step
        solved, to_p, to_n, passed = eliminate(diag[e], link[e], link[n])
        done.append(solved)
        diag[n], link[n] = minus(diag[n], to_n), passed
        if p >= 0:
            diag[p] = minus(diag[p], to_p)
        else:
            low_d = to_p if low_d is None else plus(low_d, to_p)
    d7 = minus(diag[7], keep(inner, moved(low_d, -1)))
    done4, done5, base_d, last_d, last_l = reduce_matrix(d7, link[7], pos)
    out = moved(plus(base_d, low_d), 3) + last_d + [e for r in last_l for e in r]
    for i in range(6):
        matrix_own[i] = pack_rows(out[4 * i : 4 * i + 4], 3)
    mat_copies = [
        remote(matrix_own, matrix_all.at[k], mat_send.at[i], mat_recv.at[i], p)
        for i, p in enumerate(peers)
    ]
    for copy in mat_copies:
        copy.start()
    matrix_all[k] = matrix_own[...]

    for _, comes, copy in halo[2:]:
        when(comes, copy.wait_recv)
    around = (h_left, h_right, h_below, h_rest, place)
    visc_ext = extended(visc_c, 3, *around)
    weight = stencil_weight(visc_ext)
    source = [[] for _ in range(SLICES)]
    for c in range(3):
        image = stencil(extended(v_c[c], c, *around), visc_ext, weight)
        force_c = load_slices(force, (c,))
        for v in range(SLICES):
            source[v].append(force_c[v] - image[v])
    top_source = source[7]
    ys = []
    low_s = None
    for (step, e), solved in zip(ORDER, done):
        n, p = e + step, e - step
        y, to_p, to_n = push(solved, source[e])
        ys.append(y)
        source[n] = plus(source[n], to_n)
        if p >= 0:
            source[p] = plus(source[p], to_p)
        else:
            low_s = to_p if low_s is None else plus(low_s, to_p)
    s7 = plus(source[7], keep(inner, moved(low_s, -1)))
    y4, y5, base_s, last_s = reduce_source(done4, done5, s7, pos)
    out = moved(plus(base_s, low_s), 3) + last_s
    source_own[0] = pack_rows(out[:4], 3)
    source_own[1] = pack_rows(out[4:], 3)
    src_copies = [
        remote(source_own, source_all.at[k], src_send.at[i], src_recv.at[i], p)
        for i, p in enumerate(peers)
    ]
    for copy in src_copies:
        copy.start()
    source_all[k] = source_own[...]
    for i in range(SLICES + 2):
        visc_out[i] = visc_ext[0][i]
        visc_out[SLICES + 2 + i] = visc_ext[1][i]
    for v in range(SLICES):
        visc_out[2 * SLICES + 4 + v] = weight[v]

    def gathered(ref, lo, hi, h):
        values = []
        for f in range(lo, hi):
            value = None
            for s in range(4):
                part = roll_rows(ref[2 * s + h, f // 4], s - f % 4)
                value = part if value is None else jnp.where(pos == s, part, value)
            values.append(value)
        return values

    def link_of(h):
        e = gathered(matrix_all, 12, 21, h)
        return [e[0:3], e[3:6], e[6:9]]

    for copy in mat_copies:
        copy.wait_recv()
    d0 = minus(gathered(matrix_all, 6, 12, 0), gathered(matrix_all, 0, 6, 1))
    d1 = minus(
        gathered(matrix_all, 6, 12, 1), keep(inner, moved(gathered(matrix_all, 0, 6, 0), -1))
    )
    r_h, to_p, to_n, passed = eliminate(d0, link_of(0), link_of(1))
    d1 = minus(minus(d1, to_n), keep(inner, moved(to_p, -1)))
    r4, r5, _, end_d, _ = reduce_matrix(d1, passed, pos)
    end_inv = full(sym_inverse(end_d))
    face_inv = full(sym_inverse(face[8]))
    for copy in src_copies:
        copy.wait_recv()
    s0 = plus(gathered(source_all, 3, 6, 0), gathered(source_all, 0, 3, 1))
    s1 = plus(
        gathered(source_all, 3, 6, 1), keep(inner, moved(gathered(source_all, 0, 3, 0), -1))
    )
    z_h, to_p, to_n = push(r_h, s0)
    s1 = plus(plus(s1, to_n), keep(inner, moved(to_p, -1)))
    z4, z5, _, end_s = reduce_source(r4, r5, s1, pos)
    nothing = [jnp.zeros(TILE, jnp.float32)] * 3
    x1 = expand_rows(r4, r5, z4, z5, nothing, mat_vec(end_inv, end_s), pos)
    x0 = back(r_h, z_h, keep(pos > 0, moved(x1, 1)), x1)
    own, base = nothing, nothing
    for g in range(groups):
        x = (x0, x1)[g % 2]
        own = select(k == g, moved(x, 3 - g // 2), own)
        base = select(k == g + 1, moved(x, -(g // 2)), base)
    x = [None] * SLICES
    x[7] = expand_rows(done4, done5, y4, y5, base, own, pos)
    under = select(pos == 0, base, moved(x[7], 1))
    for (step, e), solved, y in reversed(list(zip(ORDER, done, ys))):
        x[e] = back(solved, y, under if e < step else x[e - step], x[e + step])
    rhs = minus(mat_vec(full(top_diag), x[7]), mat_vec(full(face[7]), x[6]))
    over = keep(has_above, mat_vec(face_inv, minus(rhs, top_source)))
    pack_sides(ux_left, ux_right, [[x[v][c] for v in range(SLICES)] for c in range(3)])
    packed_base, packed_over = pack_rows(base, 0), pack_rows(over, 3)
    ux_left[12] = jnp.where(low, packed_base, roll_rows(packed_over, 4))
    ux_right[12] = jnp.where(low, roll_rows(packed_base, 4), packed_over)
    last = [
        (has_left, has_right, remote(ux_left, rx_right, upd_send.at[0], upd_recv.at[0], (left, k))),
        (has_right, has_left, remote(ux_right, rx_left, upd_send.at[1], upd_recv.at[1], (right, k))),
    ]
    for there, _, copy in last:
        when(there, copy.start)
    for c in range(3):
        for v in range(SLICES):
            update[8 * c + v] = x[v][c]
        ends[c] = base[c]
        ends[3 + c] = over[c]
    for there, _, copy in halo:
        when(there, copy.wait_send)
    for copy in mat_copies + src_copies:
        copy.wait_send()
    for there, comes, copy in last:
        when(comes, copy.wait_recv)
        when(there, copy.wait_send)


def image_kernel(tiles, groups, solved, ends, visc, rx_left, rx_right, update, image):
    rows, low, side_ok, has_below, has_above = edges(tiles, groups)
    pos = rows % 4
    visc_ext = ([visc[i] for i in range(10)], [visc[10 + i] for i in range(10)])
    weight = [visc[20 + v] for v in range(SLICES)]
    for c in range(3):
        x = [solved[8 * c + v] for v in range(SLICES)]
        store_slices(update, (c,), x)
        sides = []
        for m in range(4):
            lt, rt = rx_left[4 * c + m], rx_right[4 * c + m]
            sides.append(jnp.where(side_ok, jnp.where(low, lt, roll_rows(rt, 4)), 0.0))
            sides.append(jnp.where(side_ok, jnp.where(low, roll_rows(lt, 4), rt), 0.0))
        lt, rt = rx_left[12], rx_right[12]
        under = jnp.where(low, roll_rows(lt, -c), roll_rows(rt, 4 - c))
        over = jnp.where(low, roll_rows(lt, -1 - c), roll_rows(rt, 3 - c))
        centre = (
            [jnp.where(pos == 0, ends[c], roll_rows(x[7], 1))]
            + x
            + [jnp.where(pos == 3, ends[3 + c], roll_rows(x[0], -1))]
        )
        sides = (
            [jnp.where(pos == 0, jnp.where(side_ok, under, 0.0), roll_rows(sides[7], 1))]
            + sides
            + [jnp.where(pos == 3, jnp.where(side_ok, over, 0.0), roll_rows(sides[0], -1))]
        )
        store_slices(image, (c,), stencil((centre, sides), visc_ext, weight))


def tiles_of(*lead):
    return jax.ShapeDtypeStruct(lead + TILE, jnp.float32)


def per_device(tiles, groups, velocity, forcing, viscosity, fibre, inertia):
    vel, force, fib = (a.reshape(3, 64, 128) for a in (velocity, forcing, fibre))
    visc, mass = viscosity.reshape(64, 128), inertia.reshape(64, 128)
    bind = functools.partial
    vmem = pl.BlockSpec(memory_space=pltpu.VMEM)
    hbm = pl.BlockSpec(memory_space=pltpu.HBM)
    block = jax.ShapeDtypeStruct((3, 64, 128), jnp.float32)

    def space(*shape):
        return pltpu.VMEM(shape, jnp.float32)

    def tiles_in(*lead):
        return space(*lead, *TILE)

    dma = pltpu.SemaphoreType.DMA
    parts = pl.pallas_call(
        bind(solve_kernel, tiles, groups),
        out_shape=[tiles_of(n) for n in (24, 6, 28, 13, 13)],
        in_specs=[hbm] * 5,
        out_specs=[vmem] * 5,
        scratch_shapes=[
            space(3, 64, 128), space(3, 64, 128), space(64, 128), space(3, 64, 128), space(64, 128),
            tiles_in(16), tiles_in(16), tiles_in(2), tiles_in(1),
            tiles_in(16), tiles_in(16), tiles_in(2), tiles_in(5),
            tiles_in(6), tiles_in(groups, 6), tiles_in(2), tiles_in(groups, 2),
            tiles_in(13), tiles_in(13),
            dma((5,)), dma((8,)), dma((8,)),
            dma((groups - 1,)), dma((groups - 1,)), dma((groups - 1,)), dma((groups - 1,)),
            dma((2,)), dma((2,)),
        ],
        compiler_params=pltpu.CompilerParams(
            collective_id=0, has_side_effects=True, vmem_limit_bytes=67_000_000
        ),
        name="solve",
    )(vel, force, visc, fib, mass)
    update, image = pl.pallas_call(
        bind(image_kernel, tiles, groups),
        out_shape=[block, block],
        in_specs=[vmem] * 5,
        out_specs=[vmem] * 2,
        compiler_params=pltpu.CompilerParams(vmem_limit_bytes=67_000_000),
        name="image",
    )(*parts)
    return update.reshape(velocity.shape), image.reshape(velocity.shape)


def solution(mesh):
    wide, flat = P(None, "thick", "tile", None), P("thick", "tile", None)
    return jax.shard_map(
        functools.partial(per_device, mesh.shape["tile"], mesh.shape["thick"]),
        mesh=mesh,
        in_specs=(wide, wide, flat, wide, flat),
        out_specs=(wide, wide),
        check_vma=False,
    )
```

time: 45 us -> 31.9 us (0.71)
  Pallas kernels: 40.5 us -> 30.8 us
  local copies, waits for them, and re-layouts: 3.44 us -> 0 us
    pallas_call x6 -> x2, Pallas kernels: 40.5 us -> 30.8 us  [the longest x1 29 us: per_device(): pl.pallas_call(bind(solve_kernel, tiles, groups), out_shape=[tiles_of(n)...]
    unnamed x16 -> x0, local copies, waits for them, and re-layouts: 3.44 us -> none
where the time goes in v1:
time: 31.9 us; the launch traced here: 31.5 us
  Pallas kernels  30.8 us (97%)
  between operations  0.64 us (2%)
    pallas_call x1, Pallas kernels, per_device(): pl.pallas_call(bind(solve_kernel, tiles, groups), out_shape=[tiles_of(n)...  29 us
    pallas_call x1, Pallas kernels, per_device(): pl.pallas_call(bind(image_kernel, tiles, groups), out_shape=[block, block...  1.85 us

profile of v1, /device:TPU:1, one launch (start us, length us, event | category | flops | bytes accessed | tf_op | source)
XLA Modules:
  0.0 31.5 jit_solution(10153737940285114738)
XLA Ops:
  0.6 29.0 %solve.1 = (f32[24,8,128]{2,1,0:T(8,128)}, f32[6,8,128]{2,1,0:T(8,128)}, f32[28,8,128]{2,1,0:T(8,128)}, f32[13,8,128]{2,1,0:T(8,128)}, f32[13,8,128]{2,1,0:T(8,128)}) custom-call(f32[3,64,128]{2,1,0:T(8,128)} %bitcast.7, f32[3,64,128]{2,1,0:T(8,128)} %bitcast.8, f32[64,128]{1,0:T(8,128)} %bitcast.10, f32[3,64,128]{2,1,0:T(8,128)} %bitcast.9, f32[64,128]{1,0:T(8,128)} %bitcast.11), custom_call_target="tpu_custom_call" | custom-call | tf_op jit(solution)/shard_map/solve/pallas_call | solution.py:531
  29.6 1.9 %image.1 = (f32[3,64,128]{2,1,0:T(8,128)}, f32[3,64,128]{2,1,0:T(8,128)}) custom-call(f32[24,8,128]{2,1,0:T(8,128)} %get-tuple-element.9.solved, f32[6,8,128]{2,1,0:T(8,128)} %get-tuple-element.10.ends, f32[28,8,128]{2,1,0:T(8,128)} %get-tuple-element.11.visc, f32[13,8,128]{2,1,0:T(8,128)} %get-tuple-element.12.rx_left, f32[13,8,128]{2,1,0:T(8,128)} %get-tuple-element.13.rx_right), custom_call_target="tpu_custom_call" | custom-call | tf_op jit(solution)/shard_map/image/pallas_call | solution.py:551

commit v2 on v1

--- a/solution.py
+++ b/solution.py
@@ -262,7 +262,7 @@
     vel, force, visc, fibre, mass, tx_left, tx_right, tx_top, tx_bot,
     h_left, h_right, h_below, h_rest, matrix_own, matrix_all, source_own, source_all,
     ux_left, ux_right, load_sems, halo_send, halo_recv, mat_send, mat_recv, src_send, src_recv,
-    upd_send, upd_recv,
+    upd_send, upd_recv, relay_send, relay_recv,
 ):
     t, k = lax.axis_index("tile"), lax.axis_index("thick")
     loads = [
@@ -277,7 +277,10 @@
     left, right = jnp.maximum(t - 1, 0), jnp.minimum(t + 1, tiles - 1)
     down, up = jnp.maximum(k - 1, 0), jnp.minimum(k + 1, groups - 1)
     both = jnp.logical_and
-    peers = [(t, lax.rem(k + d, groups)) for d in range(1, groups)]
+    half = groups // 2
+    ring = [d for j in range(half, 0, -1) for d in sorted({j, groups - j})]
+    peers = [(t, lax.rem(k + d, groups)) for d in ring]
+    above, below = (t, lax.rem(k + 1, groups)), (t, lax.rem(k + groups - 1, groups))
     corner = tx_top.at[pl.ds(0, 1)]
     rest = [h_rest.at[pl.ds(i, 1)] for i in range(5)]
     plan = [
@@ -360,7 +363,13 @@
         matrix_own[i] = pack_rows(out[4 * i : 4 * i + 4], 3)
     mat_copies = [
         remote(matrix_own, matrix_all.at[k], mat_send.at[i], mat_recv.at[i], p)
-        for i, p in enumerate(peers)
+        for i, p in enumerate(peers[1:])
+    ]
+    passed_up = matrix_all.at[lax.rem(k + groups - half + 1, groups), pl.ds(0, 3)]
+    passed_down = matrix_all.at[lax.rem(k + half - 1, groups), pl.ds(3, 3)]
+    relays = [
+        remote(passed_up, passed_up, relay_send.at[0], relay_recv.at[0], above),
+        remote(passed_down, passed_down, relay_send.at[1], relay_recv.at[1], below),
     ]
     for copy in mat_copies:
         copy.start()
@@ -407,6 +416,10 @@
     for v in range(SLICES):
         visc_out[2 * SLICES + 4 + v] = weight[v]
 
+    for copy, relay in zip(mat_copies[:2], relays):
+        copy.wait_recv()
+        relay.start()
+
     def gathered(ref, lo, hi, h):
         values = []
         for f in range(lo, hi):
@@ -421,7 +434,7 @@
         e = gathered(matrix_all, 12, 21, h)
         return [e[0:3], e[3:6], e[6:9]]
 
-    for copy in mat_copies:
+    for copy in mat_copies[2:] + relays:
         copy.wait_recv()
     d0 = minus(gathered(matrix_all, 6, 12, 0), gathered(matrix_all, 0, 6, 1))
     d1 = minus(
@@ -473,7 +486,7 @@
         ends[3 + c] = over[c]
     for there, _, copy in halo:
         when(there, copy.wait_send)
-    for copy in mat_copies + src_copies:
+    for copy in mat_copies + relays + src_copies:
         copy.wait_send()
     for there, comes, copy in last:
         when(comes, copy.wait_recv)
@@ -540,8 +553,8 @@
             tiles_in(6), tiles_in(groups, 6), tiles_in(2), tiles_in(groups, 2),
             tiles_in(13), tiles_in(13),
             dma((5,)), dma((8,)), dma((8,)),
-            dma((groups - 1,)), dma((groups - 1,)), dma((groups - 1,)), dma((groups - 1,)),
-            dma((2,)), dma((2,)),
+            dma((groups - 2,)), dma((groups - 2,)), dma((groups - 1,)), dma((groups - 1,)),
+            dma((2,)), dma((2,)), dma((2,)), dma((2,)),
         ],
         compiler_params=pltpu.CompilerParams(
             collective_id=0, has_side_effects=True, vmem_limit_bytes=67_000_000

time: 31.9 us -> 31.8 us (level)
  the two profiles are of different devices: /device:TPU:1 before, /device:TPU:31 now
where the time goes in v2:
time: 31.8 us; the launch traced here: 31.6 us
  Pallas kernels  30.9 us (97%)
  between operations  0.64 us (2%)
    pallas_call x1, Pallas kernels, per_device(): pl.pallas_call(bind(solve_kernel, tiles, groups), out_shape=[tiles_of(n)...  29.1 us
    pallas_call x1, Pallas kernels, per_device(): pl.pallas_call(bind(image_kernel, tiles, groups), out_shape=[block, block...  1.85 us

profile of v2, /device:TPU:31, one launch (start us, length us, event | category | flops | bytes accessed | tf_op | source)
XLA Modules:
  0.0 31.6 jit_solution(3329604461649041777)
XLA Ops:
  0.6 29.1 %solve.1 = (f32[24,8,128]{2,1,0:T(8,128)}, f32[6,8,128]{2,1,0:T(8,128)}, f32[28,8,128]{2,1,0:T(8,128)}, f32[13,8,128]{2,1,0:T(8,128)}, f32[13,8,128]{2,1,0:T(8,128)}) custom-call(f32[3,64,128]{2,1,0:T(8,128)} %bitcast.7, f32[3,64,128]{2,1,0:T(8,128)} %bitcast.8, f32[64,128]{1,0:T(8,128)} %bitcast.10, f32[3,64,128]{2,1,0:T(8,128)} %bitcast.9, f32[64,128]{1,0:T(8,128)} %bitcast.11), custom_call_target="tpu_custom_call" | custom-call | tf_op jit(solution)/shard_map/solve/pallas_call | solution.py:544
  29.7 1.9 %image.1 = (f32[3,64,128]{2,1,0:T(8,128)}, f32[3,64,128]{2,1,0:T(8,128)}) custom-call(f32[24,8,128]{2,1,0:T(8,128)} %get-tuple-element.9.solved, f32[6,8,128]{2,1,0:T(8,128)} %get-tuple-element.10.ends, f32[28,8,128]{2,1,0:T(8,128)} %get-tuple-element.11.visc, f32[13,8,128]{2,1,0:T(8,128)} %get-tuple-element.12.rx_left, f32[13,8,128]{2,1,0:T(8,128)} %get-tuple-element.13.rx_right), custom_call_target="tpu_custom_call" | custom-call | tf_op jit(solution)/shard_map/image/pallas_call | solution.py:564

commit v3 on v2

--- a/solution.py
+++ b/solution.py
@@ -262,7 +262,7 @@
     vel, force, visc, fibre, mass, tx_left, tx_right, tx_top, tx_bot,
     h_left, h_right, h_below, h_rest, matrix_own, matrix_all, source_own, source_all,
     ux_left, ux_right, load_sems, halo_send, halo_recv, mat_send, mat_recv, src_send, src_recv,
-    upd_send, upd_recv, relay_send, relay_recv,
+    upd_send, upd_recv, relay_send, relay_recv, reach_sems,
 ):
     t, k = lax.axis_index("tile"), lax.axis_index("thick")
     loads = [
@@ -293,7 +293,18 @@
         ((right, down), both(has_right, has_down), both(has_left, has_up), tx_bot, rest[3]),
         ((left, down), both(has_left, has_down), both(has_right, has_up), tx_bot, rest[4]),
     ]
-    all_here = greet([(p[0], p[1]) for p in plan[2:]] + [(p, None) for p in peers])
+    near_here = greet([(p[0], p[1]) for p in plan[2:]] + [(above, None), (below, None)])
+
+    def tell(r):
+        for side, target in enumerate((above, below)):
+            pl.semaphore_signal(
+                reach_sems.at[2 * r + side], inc=1, device_id=target, device_id_type=MESH
+            )
+
+    def told(r):
+        for side in (0, 1):
+            pl.semaphore_wait(reach_sems.at[2 * r + side], 1)
+
     halo = [
         (there, comes, remote(src, dst, halo_send.at[i], halo_recv.at[i], target))
         for i, (target, there, comes, src, dst) in enumerate(plan)
@@ -308,9 +319,13 @@
     tx_top[0] = pack_rows([f[7] for f in fields], 3)
     tx_top[1] = pack_rows([f[7] for f in fib], 3)
     pack_sides(tx_left, tx_right, fields)
-    all_here()
+    near_here()
     for there, _, copy in halo:
         when(there, copy.start)
+    for r in range(half - 2):
+        tell(r)
+        told(r)
+    tell(half - 2)
     place = edges(tiles, groups)
     rows, low, side_ok, has_below, has_above = place
     pos = rows % 4
@@ -371,6 +386,7 @@
         remote(passed_up, passed_up, relay_send.at[0], relay_recv.at[0], above),
         remote(passed_down, passed_down, relay_send.at[1], relay_recv.at[1], below),
     ]
+    told(half - 2)
     for copy in mat_copies:
         copy.start()
     matrix_all[k] = matrix_own[...]
@@ -493,14 +509,19 @@
         when(there, copy.wait_send)
 
 
-def image_kernel(tiles, groups, solved, ends, visc, rx_left, rx_right, update, image):
+def image_kernel(
+    tiles, groups, solved, ends, visc, rx_left, rx_right, update_out, image_out, update, image, sems
+):
+    for c in range(3):
+        store_slices(update, (c,), [solved[8 * c + v] for v in range(SLICES)])
+    copies = [pltpu.make_async_copy(update, update_out, sems.at[3])]
+    copies[0].start()
     rows, low, side_ok, has_below, has_above = edges(tiles, groups)
     pos = rows % 4
     visc_ext = ([visc[i] for i in range(10)], [visc[10 + i] for i in range(10)])
     weight = [visc[20 + v] for v in range(SLICES)]
     for c in range(3):
         x = [solved[8 * c + v] for v in range(SLICES)]
-        store_slices(update, (c,), x)
         sides = []
         for m in range(4):
             lt, rt = rx_left[4 * c + m], rx_right[4 * c + m]
@@ -520,6 +541,10 @@
             + [jnp.where(pos == 3, jnp.where(side_ok, over, 0.0), roll_rows(sides[0], -1))]
         )
         store_slices(image, (c,), stencil((centre, sides), visc_ext, weight))
+        copies.append(pltpu.make_async_copy(image.at[c], image_out.at[c], sems.at[c]))
+        copies[-1].start()
+    for copy in copies:
+        copy.wait()
 
 
 def tiles_of(*lead):
@@ -541,6 +566,7 @@
         return space(*lead, *TILE)
 
     dma = pltpu.SemaphoreType.DMA
+    inputs = [pltpu.with_memory_space_constraint(a, pltpu.HBM) for a in (vel, force, visc, fib, mass)]
     parts = pl.pallas_call(
         bind(solve_kernel, tiles, groups),
         out_shape=[tiles_of(n) for n in (24, 6, 28, 13, 13)],
@@ -555,18 +581,20 @@
             dma((5,)), dma((8,)), dma((8,)),
             dma((groups - 2,)), dma((groups - 2,)), dma((groups - 1,)), dma((groups - 1,)),
             dma((2,)), dma((2,)), dma((2,)), dma((2,)),
+            pltpu.SemaphoreType.REGULAR((groups - 2,)),
         ],
         compiler_params=pltpu.CompilerParams(
-            collective_id=0, has_side_effects=True, vmem_limit_bytes=67_000_000
+            collective_id=0, has_side_effects=True, vmem_limit_bytes=16 * 1024 * 1024
         ),
         name="solve",
-    )(vel, force, visc, fib, mass)
+    )(*inputs)
     update, image = pl.pallas_call(
         bind(image_kernel, tiles, groups),
         out_shape=[block, block],
         in_specs=[vmem] * 5,
-        out_specs=[vmem] * 2,
-        compiler_params=pltpu.CompilerParams(vmem_limit_bytes=67_000_000),
+        out_specs=[hbm] * 2,
+        scratch_shapes=[space(3, 64, 128), space(3, 64, 128), dma((4,))],
+        compiler_params=pltpu.CompilerParams(vmem_limit_bytes=16 * 1024 * 1024),
         name="image",
     )(*parts)
     return update.reshape(velocity.shape), image.reshape(velocity.shape)

time: 31.8 us -> 28.8 us (0.906)
  the two profiles are of different devices: /device:TPU:31 before, /device:TPU:1 now
where the time goes in v3:
time: 28.8 us; the launch traced here: 28.6 us
  Pallas kernels  28 us (97%)
  between operations  0.64 us (2%)
    pallas_call x1, Pallas kernels, per_device(): pl.pallas_call(bind(solve_kernel, tiles, groups), out_shape=[tiles_of(n)...  27.1 us
    pallas_call x1, Pallas kernels, per_device(): pl.pallas_call(bind(image_kernel, tiles, groups), out_shape=[block, block...  0.88 us

profile of v3, /device:TPU:1, one launch (start us, length us, event | category | flops | bytes accessed | tf_op | source)
XLA Modules:
  0.0 28.6 jit_solution(9132737228491372506)
XLA Ops:
  0.6 27.1 %solve.1 = (f32[24,8,128]{2,1,0:T(8,128)S(1)}, f32[6,8,128]{2,1,0:T(8,128)S(1)}, f32[28,8,128]{2,1,0:T(8,128)S(1)}, f32[13,8,128]{2,1,0:T(8,128)S(1)}, f32[13,8,128]{2,1,0:T(8,128)S(1)}) custom-call(f32[3,64,128]{2,1,0:T(8,128)} %bitcast.7, f32[3,64,128]{2,1,0:T(8,128)} %bitcast.8, f32[64,128]{1,0:T(8,128)} %bitcast.10, f32[3,64,128]{2,1,0:T(8,128)} %bitcast.9, ...), custom_call_target="tpu_custom_call" | custom-call | tf_op jit(solution)/shard_map/solve/pallas_call | solution.py:570
  27.7 0.9 %image.1 = (f32[3,64,128]{2,1,0:T(8,128)}, f32[3,64,128]{2,1,0:T(8,128)}) custom-call(f32[24,8,128]{2,1,0:T(8,128)S(1)} %get-tuple-element.9.solved, f32[6,8,128]{2,1,0:T(8,128)S(1)} %get-tuple-element.10.ends, f32[28,8,128]{2,1,0:T(8,128)S(1)} %get-tuple-element.11.visc, f32[13,8,128]{2,1,0:T(8,128)S(1)} %get-tuple-element.12.rx_left, ...), custom_call_target="tpu_custom_call" | custom-call | tf_op jit(solution)/shard_map/image/pallas_call | solution.py:591

commit v4 on v3

--- a/solution.py
+++ b/solution.py
@@ -43,13 +43,15 @@
     return packed
 
 
-def pack_sides(left_ref, right_ref, fields):
+def pack_side(ref, side, fields):
     low = row_ids() < 4
     for j, slices in enumerate(fields):
         for m in range(4):
             first, second = slices[2 * m], slices[2 * m + 1]
-            left_ref[4 * j + m] = jnp.where(low, first, roll_rows(second, 4))
-            right_ref[4 * j + m] = jnp.where(low, roll_rows(first, 4), second)
+            if side == 0:
+                ref[4 * j + m] = jnp.where(low, first, roll_rows(second, 4))
+            else:
+                ref[4 * j + m] = jnp.where(low, roll_rows(first, 4), second)
 
 
 def greet(targets):
@@ -286,12 +288,12 @@
     plan = [
         ((t, up), has_up, has_down, tx_top, h_below),
         ((t, down), has_down, has_up, tx_bot, rest[0]),
-        ((left, k), has_left, has_right, tx_left, h_right),
-        ((right, k), has_right, has_left, tx_right, h_left),
         ((right, up), both(has_right, has_up), both(has_left, has_down), corner, rest[1]),
         ((left, up), both(has_left, has_up), both(has_right, has_down), corner, rest[2]),
         ((right, down), both(has_right, has_down), both(has_left, has_up), tx_bot, rest[3]),
         ((left, down), both(has_left, has_down), both(has_right, has_up), tx_bot, rest[4]),
+        ((left, k), has_left, has_right, tx_left, h_right),
+        ((right, k), has_right, has_left, tx_right, h_left),
     ]
     near_here = greet([(p[0], p[1]) for p in plan[2:]] + [(above, None), (below, None)])
 
@@ -318,9 +320,12 @@
     tx_bot[0] = pack_rows([f[0] for f in fields], 0)
     tx_top[0] = pack_rows([f[7] for f in fields], 3)
     tx_top[1] = pack_rows([f[7] for f in fib], 3)
-    pack_sides(tx_left, tx_right, fields)
     near_here()
-    for there, _, copy in halo:
+    for there, _, copy in halo[:6]:
+        when(there, copy.start)
+    for side, ref in enumerate((tx_left, tx_right)):
+        pack_side(ref, side, fields)
+        there, _, copy = halo[6 + side]
         when(there, copy.start)
     for r in range(half - 2):
         tell(r)
@@ -485,7 +490,6 @@
         x[e] = back(solved, y, under if e < step else x[e - step], x[e + step])
     rhs = minus(mat_vec(full(top_diag), x[7]), mat_vec(full(face[7]), x[6]))
     over = keep(has_above, mat_vec(face_inv, minus(rhs, top_source)))
-    pack_sides(ux_left, ux_right, [[x[v][c] for v in range(SLICES)] for c in range(3)])
     packed_base, packed_over = pack_rows(base, 0), pack_rows(over, 3)
     ux_left[12] = jnp.where(low, packed_base, roll_rows(packed_over, 4))
     ux_right[12] = jnp.where(low, roll_rows(packed_base, 4), packed_over)
@@ -493,7 +497,10 @@
         (has_left, has_right, remote(ux_left, rx_right, upd_send.at[0], upd_recv.at[0], (left, k))),
         (has_right, has_left, remote(ux_right, rx_left, upd_send.at[1], upd_recv.at[1], (right, k))),
     ]
-    for there, _, copy in last:
+    fields = [[x[v][c] for v in range(SLICES)] for c in range(3)]
+    for side, ref in enumerate((ux_left, ux_right)):
+        pack_side(ref, side, fields)
+        there, _, copy = last[side]
         when(there, copy.start)
     for c in range(3):
         for v in range(SLICES):

time: 28.8 us -> 28.8 us (level)
  no operation moved by 1% of the time
where the time goes in v4:
time: 28.8 us; the launch traced here: 28.5 us
  Pallas kernels  27.9 us (97%)
  between operations  0.64 us (2%)
    pallas_call x1, Pallas kernels, per_device(): pl.pallas_call(bind(solve_kernel, tiles, groups), out_shape=[tiles_of(n)...  27 us
    pallas_call x1, Pallas kernels, per_device(): pl.pallas_call(bind(image_kernel, tiles, groups), out_shape=[block, block...  0.88 us

profile of v4, /device:TPU:1, one launch (start us, length us, event | category | flops | bytes accessed | tf_op | source)
XLA Modules:
  0.0 28.5 jit_solution(14682621088623831037)
XLA Ops:
  0.6 27.0 %solve.1 = (f32[24,8,128]{2,1,0:T(8,128)S(1)}, f32[6,8,128]{2,1,0:T(8,128)S(1)}, f32[28,8,128]{2,1,0:T(8,128)S(1)}, f32[13,8,128]{2,1,0:T(8,128)S(1)}, f32[13,8,128]{2,1,0:T(8,128)S(1)}) custom-call(f32[3,64,128]{2,1,0:T(8,128)} %bitcast.7, f32[3,64,128]{2,1,0:T(8,128)} %bitcast.8, f32[64,128]{1,0:T(8,128)} %bitcast.10, f32[3,64,128]{2,1,0:T(8,128)} %bitcast.9, ...), custom_call_target="tpu_custom_call" | custom-call | tf_op jit(solution)/shard_map/solve/pallas_call | solution.py:577
  27.6 0.9 %image.1 = (f32[3,64,128]{2,1,0:T(8,128)}, f32[3,64,128]{2,1,0:T(8,128)}) custom-call(f32[24,8,128]{2,1,0:T(8,128)S(1)} %get-tuple-element.9.solved, f32[6,8,128]{2,1,0:T(8,128)S(1)} %get-tuple-element.10.ends, f32[28,8,128]{2,1,0:T(8,128)S(1)} %get-tuple-element.11.visc, f32[13,8,128]{2,1,0:T(8,128)S(1)} %get-tuple-element.12.rx_left, ...), custom_call_target="tpu_custom_call" | custom-call | tf_op jit(solution)/shard_map/image/pallas_call | solution.py:598

commit v5 on v4

--- a/solution.py
+++ b/solution.py
@@ -292,10 +292,12 @@
         ((left, up), both(has_left, has_up), both(has_right, has_down), corner, rest[2]),
         ((right, down), both(has_right, has_down), both(has_left, has_up), tx_bot, rest[3]),
         ((left, down), both(has_left, has_down), both(has_right, has_up), tx_bot, rest[4]),
-        ((left, k), has_left, has_right, tx_left, h_right),
-        ((right, k), has_right, has_left, tx_right, h_left),
-    ]
-    near_here = greet([(p[0], p[1]) for p in plan[2:]] + [(above, None), (below, None)])
+    ]
+    for j in (3, 0, 1, 2):
+        part = pl.ds(4 * j, 4)
+        plan.append(((left, k), has_left, has_right, tx_left.at[part], h_right.at[part]))
+        plan.append(((right, k), has_right, has_left, tx_right.at[part], h_left.at[part]))
+    near_here = greet([(p[0], p[1]) for p in plan[2:8]] + [(above, None), (below, None)])
 
     def tell(r):
         for side, target in enumerate((above, below)):
@@ -323,10 +325,11 @@
     near_here()
     for there, _, copy in halo[:6]:
         when(there, copy.start)
-    for side, ref in enumerate((tx_left, tx_right)):
-        pack_side(ref, side, fields)
-        there, _, copy = halo[6 + side]
-        when(there, copy.start)
+    for i, j in enumerate((3, 0, 1, 2)):
+        for side, ref in enumerate((tx_left, tx_right)):
+            pack_side(ref.at[pl.ds(4 * j, 4)], side, [fields[j]])
+            there, _, copy = halo[6 + 2 * i + side]
+            when(there, copy.start)
     for r in range(half - 2):
         tell(r)
         told(r)
@@ -396,13 +399,15 @@
         copy.start()
     matrix_all[k] = matrix_own[...]
 
-    for _, comes, copy in halo[2:]:
+    for _, comes, copy in halo[2:8]:
         when(comes, copy.wait_recv)
     around = (h_left, h_right, h_below, h_rest, place)
     visc_ext = extended(visc_c, 3, *around)
     weight = stencil_weight(visc_ext)
     source = [[] for _ in range(SLICES)]
     for c in range(3):
+        for _, comes, copy in halo[8 + 2 * c : 10 + 2 * c]:
+            when(comes, copy.wait_recv)
         image = stencil(extended(v_c[c], c, *around), visc_ext, weight)
         force_c = load_slices(force, (c,))
         for v in range(SLICES):
@@ -585,7 +590,7 @@
             tiles_in(16), tiles_in(16), tiles_in(2), tiles_in(5),
             tiles_in(6), tiles_in(groups, 6), tiles_in(2), tiles_in(groups, 2),
             tiles_in(13), tiles_in(13),
-            dma((5,)), dma((8,)), dma((8,)),
+            dma((5,)), dma((14,)), dma((14,)),
             dma((groups - 2,)), dma((groups - 2,)), dma((groups - 1,)), dma((groups - 1,)),
             dma((2,)), dma((2,)), dma((2,)), dma((2,)),
             pltpu.SemaphoreType.REGULAR((groups - 2,)),

time: 28.8 us -> 28.8 us (level)
  no operation moved by 1% of the time
where the time goes in v5:
time: 28.8 us; the launch traced here: 28.7 us
  Pallas kernels  28 us (97%)
  between operations  0.64 us (2%)
    pallas_call x1, Pallas kernels, per_device(): pl.pallas_call(bind(solve_kernel, tiles, groups), out_shape=[tiles_of(n)...  27.1 us
    pallas_call x1, Pallas kernels, per_device(): pl.pallas_call(bind(image_kernel, tiles, groups), out_shape=[block, block...  0.88 us

profile of v5, /device:TPU:1, one launch (start us, length us, event | category | flops | bytes accessed | tf_op | source)
XLA Modules:
  0.0 28.7 jit_solution(1197492189804672563)
XLA Ops:
  0.6 27.1 %solve.1 = (f32[24,8,128]{2,1,0:T(8,128)S(1)}, f32[6,8,128]{2,1,0:T(8,128)S(1)}, f32[28,8,128]{2,1,0:T(8,128)S(1)}, f32[13,8,128]{2,1,0:T(8,128)S(1)}, f32[13,8,128]{2,1,0:T(8,128)S(1)}) custom-call(f32[3,64,128]{2,1,0:T(8,128)} %bitcast.7, f32[3,64,128]{2,1,0:T(8,128)} %bitcast.8, f32[64,128]{1,0:T(8,128)} %bitcast.10, f32[3,64,128]{2,1,0:T(8,128)} %bitcast.9, ...), custom_call_target="tpu_custom_call" | custom-call | tf_op jit(solution)/shard_map/solve/pallas_call | solution.py:582
  27.8 0.9 %image.1 = (f32[3,64,128]{2,1,0:T(8,128)}, f32[3,64,128]{2,1,0:T(8,128)}) custom-call(f32[24,8,128]{2,1,0:T(8,128)S(1)} %get-tuple-element.9.solved, f32[6,8,128]{2,1,0:T(8,128)S(1)} %get-tuple-element.10.ends, f32[28,8,128]{2,1,0:T(8,128)S(1)} %get-tuple-element.11.visc, f32[13,8,128]{2,1,0:T(8,128)S(1)} %get-tuple-element.12.rx_left, ...), custom_call_target="tpu_custom_call" | custom-call | tf_op jit(solution)/shard_map/image/pallas_call | solution.py:603

commit v6 on v5

--- a/solution.py
+++ b/solution.py
@@ -498,15 +498,19 @@
     packed_base, packed_over = pack_rows(base, 0), pack_rows(over, 3)
     ux_left[12] = jnp.where(low, packed_base, roll_rows(packed_over, 4))
     ux_right[12] = jnp.where(low, roll_rows(packed_base, 4), packed_over)
-    last = [
-        (has_left, has_right, remote(ux_left, rx_right, upd_send.at[0], upd_recv.at[0], (left, k))),
-        (has_right, has_left, remote(ux_right, rx_left, upd_send.at[1], upd_recv.at[1], (right, k))),
-    ]
-    fields = [[x[v][c] for v in range(SLICES)] for c in range(3)]
-    for side, ref in enumerate((ux_left, ux_right)):
-        pack_side(ref, side, fields)
-        there, _, copy = last[side]
-        when(there, copy.start)
+    last = []
+    for c in range(3):
+        part = pl.ds(4 * c, 5 if c == 2 else 4)
+        ways = (
+            (has_left, has_right, ux_left, rx_right, (left, k)),
+            (has_right, has_left, ux_right, rx_left, (right, k)),
+        )
+        for side, (there, comes, src, dst, target) in enumerate(ways):
+            pack_side(src.at[pl.ds(4 * c, 4)], side, [[x[v][c] for v in range(SLICES)]])
+            sems = upd_send.at[2 * c + side], upd_recv.at[2 * c + side]
+            copy = remote(src.at[part], dst.at[part], *sems, target)
+            when(there, copy.start)
+            last.append((there, comes, copy))
     for c in range(3):
         for v in range(SLICES):
             update[8 * c + v] = x[v][c]
@@ -592,7 +596,7 @@
             tiles_in(13), tiles_in(13),
             dma((5,)), dma((14,)), dma((14,)),
             dma((groups - 2,)), dma((groups - 2,)), dma((groups - 1,)), dma((groups - 1,)),
-            dma((2,)), dma((2,)), dma((2,)), dma((2,)),
+            dma((6,)), dma((6,)), dma((2,)), dma((2,)),
             pltpu.SemaphoreType.REGULAR((groups - 2,)),
         ],
         compiler_params=pltpu.CompilerParams(

time: 28.8 us -> 28.9 us (level)
  no operation moved by 1% of the time
where the time goes in v6:
time: 28.9 us; the launch traced here: 28.7 us
  Pallas kernels  28.1 us (97%)
  between operations  0.64 us (2%)
    pallas_call x1, Pallas kernels, per_device(): pl.pallas_call(bind(solve_kernel, tiles, groups), out_shape=[tiles_of(n)...  27.2 us
    pallas_call x1, Pallas kernels, per_device(): pl.pallas_call(bind(image_kernel, tiles, groups), out_shape=[block, block...  0.88 us

profile of v6, /device:TPU:1, one launch (start us, length us, event | category | flops | bytes accessed | tf_op | source)
XLA Modules:
  0.0 28.7 jit_solution(14535532871308507886)
XLA Ops:
  0.6 27.2 %solve.1 = (f32[24,8,128]{2,1,0:T(8,128)S(1)}, f32[6,8,128]{2,1,0:T(8,128)S(1)}, f32[28,8,128]{2,1,0:T(8,128)S(1)}, f32[13,8,128]{2,1,0:T(8,128)S(1)}, f32[13,8,128]{2,1,0:T(8,128)S(1)}) custom-call(f32[3,64,128]{2,1,0:T(8,128)} %bitcast.7, f32[3,64,128]{2,1,0:T(8,128)} %bitcast.8, f32[64,128]{1,0:T(8,128)} %bitcast.10, f32[3,64,128]{2,1,0:T(8,128)} %bitcast.9, ...), custom_call_target="tpu_custom_call" | custom-call | tf_op jit(solution)/shard_map/solve/pallas_call | solution.py:586
  27.8 0.9 %image.1 = (f32[3,64,128]{2,1,0:T(8,128)}, f32[3,64,128]{2,1,0:T(8,128)}) custom-call(f32[24,8,128]{2,1,0:T(8,128)S(1)} %get-tuple-element.9.solved, f32[6,8,128]{2,1,0:T(8,128)S(1)} %get-tuple-element.10.ends, f32[28,8,128]{2,1,0:T(8,128)S(1)} %get-tuple-element.11.visc, f32[13,8,128]{2,1,0:T(8,128)S(1)} %get-tuple-element.12.rx_left, ...), custom_call_target="tpu_custom_call" | custom-call | tf_op jit(solution)/shard_map/image/pallas_call | solution.py:607
